TPU v7x, 768 devices: a whole 4x8x12 slice. The times are simulated.
768 devices in a mesh: segment: 48 (over x, z), seq: 16 (over y, core).
Axes of the slice: x: 4, y: 8, z: 12, core: 2. Of those that a mesh axis runs over, the one named last changes fastest.
Arguments:
- projected: bfloat16 [48, 1024, 6144], P('segment', 'seq'), may hold values from -128 to 128
- stream_before: bfloat16 [48, 1024, 2048], P('segment', 'seq'), may hold values from -3 to 3
- out_weight: bfloat16 [48, 2048, 2048], P('segment', 'seq'), may hold values from -0.25 to 0.25
- proj_weight: bfloat16 [48, 2048, 6144], P('segment', None, 'seq'), may hold values from -0.125 to 0.125
- norm_gain: float32 [48, 2048], P('segment'), may hold values from 0.1 to 1.9
- block_mask: int32 [4, 2, 2], replicated, may hold values from 0 to 1, as said below
- token_order: int32 [1024], replicated, may hold values from 0 to 1023, each once
Outputs:
- incoming: bfloat16 [48, 1024, 2048], P('segment', 'seq')
- next_projected: bfloat16 [48, 1024, 6144], P('segment', None, 'seq')
Inputs may be any that keep to these rules, and one draw needn't show every extreme that they name: Each query block may always see the key block at its own place in the window (block_mask[w, b, b] = 1).
All inputs are finite; a program needn't handle non-finite values.
Results may differ from a plain program's by a relative error of at most 0.014.
Values may be sent and summed in bfloat16 or wider, within the bound.
A program may use at most 32 MiB of HBM per device.

v0:
```python
import jax
import jax.numpy as jnp
from jax import lax
from jax.sharding import PartitionSpec as P

HEADS = 16
DH = 128
WIN = 256
BLOCK = 128


def from_behind(x, axis, by):
    size = lax.axis_size(axis)
    return lax.ppermute(x, axis, [(i, (i + by) % size) for i in range(size)])


def normalize(values, gain):
    widened = values.astype(jnp.float32)
    scale = lax.rsqrt(jnp.mean(widened * widened, axis=-1, keepdims=True) + 1e-06)
    return (widened * scale * gain[None, :]).astype(jnp.bfloat16)


def local(projected, stream_before, out_weight, proj_weight, norm_gain, block_mask, token_order):
    group_size = lax.axis_size("seq")
    local_heads = HEADS // group_size
    tok_rows = projected.shape[1]
    all_tokens = tok_rows * group_size
    by_head = lax.all_to_all(projected[0], "seq", split_axis=1, concat_axis=0, tiled=True)
    ordered = by_head.reshape(all_tokens, local_heads, 3, DH)[token_order]
    windows = ordered.reshape(all_tokens // WIN, WIN, local_heads, 3, DH)
    allowed = jnp.repeat(jnp.repeat(block_mask, BLOCK, axis=1), BLOCK, axis=2) > 0
    scores = jnp.einsum(
        "wqhd,wkhd->whqk",
        windows[:, :, :, 0],
        windows[:, :, :, 1],
        preferred_element_type=jnp.float32,
    ) * DH ** (-0.5)
    masked = jnp.where(allowed[:, None], scores, -jnp.inf)
    highest = jnp.max(masked, axis=-1, keepdims=True)
    weights = jnp.exp(masked - highest)
    probs = (weights / jnp.sum(weights, axis=-1, keepdims=True)).astype(jnp.bfloat16)
    attended = jnp.einsum(
        "whqk,wkhd->wqhd", probs, windows[:, :, :, 2], preferred_element_type=jnp.float32
    ).astype(jnp.bfloat16)
    placed = (
        jnp.zeros((all_tokens, local_heads, DH), jnp.bfloat16)
        .at[token_order]
        .set(attended.reshape(all_tokens, local_heads, DH))
    )
    placed = placed.reshape(all_tokens, local_heads * DH)
    branch = lax.psum_scatter(
        jnp.dot(placed, out_weight[0], preferred_element_type=jnp.float32).astype(jnp.bfloat16),
        "seq",
        scatter_dimension=0,
        tiled=True,
    ).astype(jnp.float32)
    stream_after = (stream_before[0].astype(jnp.float32) + branch).astype(jnp.bfloat16)
    assembled = lax.all_gather(stream_after, "seq", axis=0, tiled=True)
    arrived = from_behind(assembled, "segment", 1)
    incoming = lax.dynamic_slice_in_dim(arrived, lax.axis_index("seq") * tok_rows, tok_rows, 0)
    normed = normalize(arrived, norm_gain[0])
    following = jnp.dot(normed, proj_weight[0], preferred_element_type=jnp.float32).astype(
        jnp.bfloat16
    )
    return (incoming[None], following[None])


def solution(mesh):
    placed = (
        P("segment", "seq", None),
        P("segment", "seq", None),
        P("segment", "seq", None),
        P("segment", None, "seq"),
        P("segment", None),
        P(),
        P(),
    )
    return jax.shard_map(
        local,
        mesh=mesh,
        in_specs=placed,
        out_specs=(P("segment", "seq", None), P("segment", None, "seq")),
        check_vma=False,
    )
```

profile of v0, /device:TPU:1, one launch (start us, length us, event | category | flops | bytes accessed | tf_op | source)
XLA Modules:
  0.0 294.6 jit_solution(14315438263240764543)
XLA Ops:
  7.2 0.0 copy-start
  7.2 0.0 copy-start.4
  7.2 0.0 copy-start.3
  7.2 1.4 copy.21
  8.6 1.1 copy.12
  9.6 13.9 %all-to-all-start = ((bf16[64,16,384]{2,0,1:T(8,128)(2,1)}), bf16[64,16,384]{2,0,1:T(8,128)(2,1)S(1)}, u32[]{:S(2)}, u32[]{:S(2)}) async-start(bf16[64,16,384]{2,0,1:T(8,128)(2,1)} %copy.12), calls=%async_computation | async-start | bytes 1572864 | tf_op jit(solution)/shard_map/all_to_all | solution.py:28
  23.5 0.0 reduce-scatter.2.cloned.1.call-start
  23.5 0.0 copy-done.4
  23.6 0.1 copy.14
  23.7 0.1 broadcast_in_dim.29
  23.8 0.0 copy-done.3
  23.8 22.5 %all-to-all-done = bf16[64,16,384]{2,0,1:T(8,128)(2,1)S(1)} async-done(((bf16[64,16,384]{2,0,1:T(8,128)(2,1)}), bf16[64,16,384]{2,0,1:T(8,128)(2,1)S(1)}, u32[]{:S(2)}, u32[]{:S(2)}) %all-to-all-start) | async-done | bytes 786464 | tf_op jit(solution)/shard_map/all_to_all | solution.py:28
  46.3 0.2 reshape.78
  46.5 7.5 %gather_fusion = bf16[1024,3,128]{2,1,0:T(4,128)(2,1)} fusion(bf16[1024,3,128]{2,1,0:T(4,128)(2,1)S(1)} %reshape.78, s32[1024]{0:T(1024)S(1)} %get-tuple-element.2), kind=kCustom, calls=%fused_computation | custom fusion | bytes 1576960 | tf_op jit(solution)/shard_map/gather | solution.py:29
  54.1 1.3 copy.13
  55.4 0.1 broadcast_in_dim.30
  55.5 0.0 copy-start.1
  55.5 0.5 fusion.34
  56.0 0.7 fusion.22
  56.8 0.2 copy.18
  56.9 3.2 %scatter_custom_fusion = bf16[1024,128]{1,0:T(8,128)(2,1)S(1)} fusion(s32[1024]{0:T(1024)S(1)} %get-tuple-element.3, bf16[1024,128]{1,0:T(8,128)(2,1)S(1)} %bitcast.66, bf16[]{:T(256)} %constant.10.clone.1), kind=kCustom, calls=%fused_computation.29 | custom fusion | bytes 262146 | tf_op jit(solution)/shard_map/scatter | solution.py:48
  60.2 0.0 copy-done.1
  60.2 0.0 copy-start.2
  60.2 3.2 %convolution_convert_fusion = bf16[1024,2048]{1,0:T(8,128)(2,1)} fusion(bf16[1024,128]{1,0:T(8,128)(2,1)S(1)} %scatter_custom_fusion, bf16[1,128,2048]{2,1,0:T(8,128)(2,1)S(1)} %copy-done.1), kind=kOutput, calls=%fused_computation.11 | convolution fusion | flops 538968064 | bytes 4980736 | tf_op jit(solution)/shard_map/dot_general | solution.py:52
  63.4 0.0 copy-start.5
  63.4 0.0 reduce-scatter.2.cloned.1.call-update
  63.4 0.0 all-gather.2.cloned.1.call-start
  63.4 64.0 %reduce-scatter.2.cloned.1.call-done = bf16[64,2048]{1,0:T(8,128)(2,1)} async-done(((bf16[1024,2048]{1,0:T(8,128)(2,1)}), bf16[64,2048]{1,0:T(8,128)(2,1)}) %reduce-scatter.2.cloned.1.call-update) | async-done | bytes 262160 | tf_op jit(solution)/shard_map/reduce_scatter | solution.py:51
  127.4 0.0 copy-done.2
  127.4 1.7 fusion.23
  129.2 0.0 all-gather.2.cloned.1.call-update
  129.2 49.0 %all-gather.2.cloned.1.call-done = bf16[1024,2048]{1,0:T(8,128)(2,1)} async-done(((bf16[64,2048]{1,0:T(8,128)(2,1)}), bf16[1024,2048]{1,0:T(8,128)(2,1)}) %all-gather.2.cloned.1.call-update) | async-done | bytes 4194320 | tf_op jit(solution)/shard_map/all_gather | solution.py:58
  178.1 3.3 %collective-permute-start = (bf16[1024,2048]{1,0:T(8,128)(2,1)}, bf16[1024,2048]{1,0:T(8,128)(2,1)}, u32[]{:S(2)}, u32[]{:S(2)}) collective-permute-start(bf16[1024,2048]{1,0:T(8,128)(2,1)} %all-gather.2.cloned.1.call-done), channel_id=1, source_target_pairs={{0,16},{16,32},{32,48},{48,64},{64,80},{80,96},{96,112},{112,128},... | collective-permute-start | bytes 12582920 | tf_op jit(solution)/shard_map/ppermute | solution.py:14
  181.4 96.1 %collective-permute-done = bf16[1024,2048]{1,0:T(8,128)(2,1)} collective-permute-done((bf16[1024,2048]{1,0:T(8,128)(2,1)}, bf16[1024,2048]{1,0:T(8,128)(2,1)}, u32[]{:S(2)}, u32[]{:S(2)}) %collective-permute-start) | collective-permute-done | bytes 4194336 | tf_op jit(solution)/shard_map/ppermute | solution.py:14
  277.5 3.1 %fusion.1 = f32[1024]{0:T(1024)S(1)} fusion(bf16[1024,2048]{1,0:T(8,128)(2,1)} %collective-permute-done), kind=kLoop, calls=%fused_computation.5 | loop fusion | flops 6290432 | bytes 4198400 | tf_op jit(solution)/shard_map/reduce_sum | solution.py:19
  280.6 1.7 dynamic-slice_bitcast_fusion
  282.3 0.0 copy-done
  282.3 0.0 copy-done.5
  282.3 5.4 %fusion.17 = bf16[1,1024,384]{2,1,0:T(8,128)(2,1)} fusion(bf16[1,2048,384]{2,1,0:T(8,128)(2,1)S(1)} %copy-done, bf16[1024,2048]{1,0:T(8,128)(2,1)} %collective-permute-done, f32[2048]{0:T(1024)S(1)} %bitcast.69, f32[1024]{0:T(1024)S(1)} %add_rsqrt_fusion), kind=kOutput, calls=%fused_computation.18 | convolution fusion | flops 1619394560 | bytes 6565888 | tf_op jit(solution)/shard_map/dot_general | solution.py:62
  (5 shorter events, 0.1 us)
Async XLA Ops:
  7.2 275.1 %copy-start = (bf16[1,2048,384]{2,1,0:T(8,128)(2,1)S(1)}, bf16[1,2048,384]{2,1,0:T(8,128)(2,1)}, u32[]{:S(2)}) copy-start(bf16[1,2048,384]{2,1,0:T(8,128)(2,1)} %param.10) | copy-start | bytes 4718596
  7.2 16.4 %copy-start.4 = (s32[4,2,2]{0,2,1:T(2,128)S(1)}, s32[4,2,2]{0,2,1:T(2,128)}, u32[]{:S(2)}) copy-start(s32[4,2,2]{0,2,1:T(2,128)} %param.12) | copy-start | bytes 196
  7.2 16.6 %copy-start.3 = (s32[1024]{0:T(1024)S(1)}, s32[1024]{0:T(1024)}, u32[]{:S(2)}) copy-start(s32[1024]{0:T(1024)} %param.13) | copy-start | bytes 12292
  9.6 36.7 %all-to-all-start = ((bf16[64,16,384]{2,0,1:T(8,128)(2,1)}), bf16[64,16,384]{2,0,1:T(8,128)(2,1)S(1)}, u32[]{:S(2)}, u32[]{:S(2)}) async-start(bf16[64,16,384]{2,0,1:T(8,128)(2,1)} %copy.12), calls=%async_computation | async-start | bytes 1572864 | tf_op jit(solution)/shard_map/all_to_all | solution.py:28
  23.5 103.9 %reduce-scatter.2.cloned.1.call-start = ((), (), s32[]{:S(2)}) async-start(), calls=%async_computation.2 | async-start | bytes 4456448 | tf_op jit(solution)/shard_map/reduce_scatter | solution.py:51
  55.5 4.7 %copy-start.1 = (bf16[1,128,2048]{2,1,0:T(8,128)(2,1)S(1)}, bf16[1,128,2048]{2,1,0:T(8,128)(2,1)}, u32[]{:S(2)}) copy-start(bf16[1,128,2048]{2,1,0:T(8,128)(2,1)} %param.9) | copy-start | bytes 1572868
  60.2 67.3 %copy-start.2 = (bf16[1,64,2048]{2,1,0:T(8,128)(2,1)S(1)}, bf16[1,64,2048]{2,1,0:T(8,128)(2,1)}, u32[]{:S(2)}) copy-start(bf16[1,64,2048]{2,1,0:T(8,128)(2,1)} %param.8) | copy-start | bytes 786436
  63.4 218.9 %copy-start.5 = (f32[1,2048]{1,0:T(1,128)S(1)}, f32[1,2048]{1,0:T(1,128)}, u32[]{:S(2)}) copy-start(f32[1,2048]{1,0:T(1,128)} %param.11) | copy-start | bytes 24580
  63.4 114.7 %all-gather.2.cloned.1.call-start = ((), (), s32[]{:S(2)}) async-start(), calls=%async_computation.3 | async-start | bytes 4456448 | tf_op jit(solution)/shard_map/all_gather | solution.py:58
  178.1 99.4 %collective-permute-start = (bf16[1024,2048]{1,0:T(8,128)(2,1)}, bf16[1024,2048]{1,0:T(8,128)(2,1)}, u32[]{:S(2)}, u32[]{:S(2)}) collective-permute-start(bf16[1024,2048]{1,0:T(8,128)(2,1)} %all-gather.2.cloned.1.call-done), channel_id=1, source_target_pairs={{0,16},{16,32},{32,48},{48,64},{64,80},{80,96},{96,112},{112,128},... | collective-permute-start | bytes 12582920 | tf_op jit(solution)/shard_map/ppermute | solution.py:14
Sparse Core Ops, SparseCore 0:
  63.5 63.8 reduce-scatter.1
  130.4 47.6 all-gather.1
where the time goes:
time: 295 us
  waiting for transfers between devices  232 us (79%)
  starting transfers between devices  17.2 us (6%)
  local copies, waits for them, and re-layouts  16.9 us (6%)
  between operations  14.2 us (5%)
  matrix products  9.87 us (3%)
  other arithmetic  4.81 us (2%)
    ppermute x1, waiting for transfers between devices, from_behind(): return lax.ppermute(x, axis, [(i, (i + by) % size) for i in range(size)])  96.1 us
    reduce_scatter x1, waiting for transfers between devices, local(): lax.psum_scatter(jnp.dot(placed, out_weight[0], preferred_element_type=jn...  64 us
    all_gather x1, waiting for transfers between devices, local(): assembled = lax.all_gather(stream_after, 'seq', axis=0, tiled=True)  49 us
    all_to_all x1, waiting for transfers between devices, local(): lax.all_to_all(projected[0], 'seq', split_axis=1, concat_axis=0, tiled=True)  22.5 us
    all_to_all x1, starting transfers between devices, local(): lax.all_to_all(projected[0], 'seq', split_axis=1, concat_axis=0, tiled=True)  13.9 us
    gather x2, local copies, waits for them, and re-layouts, local(): ordered = by_head.reshape(all_tokens, local_heads, 3, DH)[token_order]  8.87 us
  transfers between devices with their start and end apart: 4, of which 4 were waited for; matrix products, arithmetic and copies ran while one was open for 0% of the time, Pallas kernels for 0%

commit v1 on v0

v1 whole, which is shorter than its diff:
```python
import functools

import jax
import jax.numpy as jnp
from jax import lax
from jax.experimental import pallas as pl
from jax.experimental.pallas import tpu as pltpu
from jax.sharding import PartitionSpec as P

DH = 128
WIN = 256
BLOCK = 128
LANES = 128
SUBS = 4
COLS = 512
HIDDEN = -1e30
BF = jnp.bfloat16
F32 = jnp.float32


def remote(src, dst, send_sem, recv_sem, device):
    return pltpu.make_async_remote_copy(
        src_ref=src,
        dst_ref=dst,
        send_sem=send_sem,
        recv_sem=recv_sem,
        device_id=device,
        device_id_type=pl.DeviceIdType.MESH,
    )


def kernel(
    n_seg, n_seq,
    order_ref, mask_ref, gain_ref, projected, stream_before, out_weight, proj_weight,
    incoming_ref, next_ref,
    qkv, perm, unperm, bias, att, placed, gathered, weight, stream, wide, total,
    rs_out, rs_in, mine, theirs,
    own_sem, pw_sem, qkv_send, qkv_recv, w_send, w_recv, wp_send, wp_recv, st_send, st_recv,
    att_send, att_recv, rs_send, rs_recv, ag_send, ag_recv, pr_send, pr_recv,
):
    n_chips = n_seq // 2
    rows, width = stream.shape
    tokens = rows * n_seq
    part = rows // SUBS
    head_cols = 3 * DH
    seg, me = lax.axis_index("segment"), lax.axis_index("seq")
    core, chip = lax.rem(me, 2), me // 2
    turn = 1 - 2 * core
    ahead = {"seq": lax.rem(chip + turn + n_chips, n_chips) * 2 + core}
    peer = {"seq": chip * 2 + 1 - core}
    seg_next, seg_last = lax.rem(seg + 1, n_seg), lax.rem(seg + n_seg - 1, n_seg)

    barrier = pltpu.get_barrier_semaphore()
    for i in range(1, n_seq):
        pl.semaphore_signal(
            barrier, inc=1, device_id={"seq": lax.rem(me + i, n_seq)},
            device_id_type=pl.DeviceIdType.MESH,
        )
    for other in (seg_next, seg_last):
        for k in range(2):
            pl.semaphore_signal(
                barrier, inc=1, device_id={"segment": other, "seq": chip * 2 + k},
                device_id_type=pl.DeviceIdType.MESH,
            )

    def block_of(j):
        return projected.at[:, pl.ds(pl.multiple_of(j * head_cols, LANES), head_cols)]

    own = pltpu.make_async_copy(block_of(me), qkv.at[me], own_sem)
    own.start()
    wide_copy = pltpu.make_async_copy(proj_weight, wide, pw_sem)
    wide_copy.start()

    pl.semaphore_wait(barrier, n_seq + 3)

    def exchange(j):
        return remote(block_of(j), qkv.at[me], qkv_send.at[j], qkv_recv.at[me], {"seq": j})

    steps = [n_chips // 2]
    for d in range(n_chips // 2 - 1, 0, -1):
        steps += [d, n_chips - d]
    for d in steps:
        for k in range(2):
            exchange(lax.rem(chip + d, n_chips) * 2 + k).start()
    exchange(chip * 2 + 1 - core).start()
    straight = {"segment": seg_next, "seq": me}
    weight_out = remote(out_weight, weight.at[core], w_send, w_recv, straight)
    weight_out.start()
    stream_out = remote(stream_before, stream, st_send, st_recv, straight)
    stream_out.start()

    tiles = tokens // LANES
    order = order_ref[...]

    for q in range(tiles):
        spread = jnp.broadcast_to(order[q : q + 1, :], (LANES, LANES)).astype(F32)
        column = jnp.transpose(spread)
        for r in range(tiles):
            there = lax.broadcasted_iota(jnp.int32, (LANES, LANES), 1) + r * LANES
            perm[q * LANES : (q + 1) * LANES, r * LANES : (r + 1) * LANES] = jnp.where(
                column == there.astype(F32), 1.0, 0.0
            ).astype(BF)

    @pl.loop(0, n_seq)
    def _(b):
        base = lax.rem(b, n_chips) * (2 * rows) + (b // n_chips) * rows
        there = lax.broadcasted_iota(jnp.int32, (rows, LANES), 0) + base
        for q in range(tiles):
            here = jnp.broadcast_to(order[q : q + 1, :], (rows, LANES))
            unperm[b, :, q * LANES : (q + 1) * LANES] = jnp.where(
                here == there, 1.0, 0.0
            ).astype(BF)

    for w in range(tokens // WIN):
        for a in range(WIN // BLOCK):
            for b in range(WIN // BLOCK):
                seen = mask_ref[(w * (WIN // BLOCK) + a) * (WIN // BLOCK) + b]
                level = (1 - jnp.minimum(seen, 1)).astype(F32) * HIDDEN
                bias[w, a * BLOCK : (a + 1) * BLOCK, b * BLOCK : (b + 1) * BLOCK] = (
                    jnp.zeros((BLOCK, BLOCK), F32) + level
                )

    weight_out.wait_recv()
    weight_pair = remote(weight.at[core], weight.at[core], wp_send, wp_recv, peer)
    weight_pair.start()
    own.wait()

    @pl.loop(1, n_seq)
    def _(i):
        j = lax.rem(me + i, n_seq)
        remote(qkv.at[j], qkv.at[j], qkv_send.at[j], qkv_recv.at[j], {"seq": j}).wait_recv()

    for w in range(tokens // WIN):
        seen = slice(w * WIN, (w + 1) * WIN)
        picked = jnp.dot(
            perm[seen, :], qkv[...].reshape(tokens, head_cols), preferred_element_type=F32
        ).astype(BF)
        scores = lax.dot_general(
            picked[:, :DH], picked[:, DH : 2 * DH], (((1,), (1,)), ((), ())),
            preferred_element_type=F32,
        )
        scores = scores * DH ** (-0.5) + bias[w]
        highest = jnp.max(scores, axis=-1, keepdims=True)
        raised = jnp.exp(scores - highest)
        probs = (raised / jnp.sum(raised, axis=-1, keepdims=True)).astype(BF)
        att[seen, :] = jnp.dot(probs, picked[:, 2 * DH :], preferred_element_type=F32).astype(BF)

    def hand_on(t, k):
        return remote(
            placed.at[t, pl.ds(k * rows, rows)], gathered.at[core, t],
            att_send.at[t, k], att_recv.at[core, t],
            {"segment": seg_next, "seq": chip * 2 + k},
        )

    @pl.loop(0, n_chips)
    def _(t):
        up = lax.rem(chip + 2 * n_chips - 1 - t, n_chips)
        down = lax.rem(chip + 1 + t, n_chips)
        both = jnp.concatenate([unperm[up], unperm[n_chips + down]], axis=0)
        placed[t] = jnp.dot(both, att[...], preferred_element_type=F32).astype(BF)
        for k in range(2):
            hand_on(t, k).start()

    other_weight = remote(
        weight.at[1 - core], weight.at[1 - core], wp_send, wp_recv, peer
    )
    other_weight.wait_recv()

    def term(t):
        for k in range(2):
            remote(
                gathered.at[k, t], gathered.at[k, t], att_send.at[t, k], att_recv.at[k, t], peer
            ).wait_recv()
        left = jnp.concatenate([gathered[0, t], gathered[1, t]], axis=1)
        for n in range(width // COLS):
            cut = slice(n * COLS, (n + 1) * COLS)
            total[:, cut] = jnp.dot(
                left, weight[:, :, cut].reshape(2 * DH, COLS), preferred_element_type=F32
            )

    def reduce_on(t, s):
        cut = pl.ds(s * part, part)
        return remote(
            rs_out.at[t, cut], rs_in.at[t, cut], rs_send.at[t, s], rs_recv.at[t, s], ahead
        )

    term(0)
    for s in range(SUBS):
        cut = pl.ds(s * part, part)
        rs_out[0, cut, :] = total[cut, :].astype(BF)
        reduce_on(0, s).start()

    @pl.loop(1, n_chips - 1)
    def _(t):
        term(t)
        for s in range(SUBS):
            cut = pl.ds(s * part, part)
            reduce_on(t - 1, s).wait_recv()
            rs_out[t, cut, :] = (total[cut, :] + rs_in[t - 1, cut, :].astype(F32)).astype(BF)
            reduce_on(t, s).start()

    def gather_on(t, s):
        cut = pl.ds(s * part, part)
        return remote(
            mine.at[t, cut], mine.at[t + 1, cut], ag_send.at[t, s], ag_recv.at[t, s], ahead
        )

    def share(t, s):
        cut = pl.ds(s * part, part)
        return remote(
            mine.at[t, cut], theirs.at[t, cut], pr_send.at[t, s], pr_recv.at[t, s], peer
        )

    term(n_chips - 1)
    stream_out.wait_recv()
    for s in range(SUBS):
        cut = pl.ds(s * part, part)
        reduce_on(n_chips - 2, s).wait_recv()
        branch = total[cut, :] + rs_in[n_chips - 2, cut, :].astype(F32)
        after = (stream[cut, :].astype(F32) + branch).astype(BF)
        incoming_ref[cut, :] = after
        widened = after.astype(F32)
        scale = lax.rsqrt(jnp.mean(widened * widened, axis=-1, keepdims=True) + 1e-06)
        mine[0, cut, :] = (widened * scale * gain_ref[...]).astype(BF)
        gather_on(0, s).start()
        share(0, s).start()

    wide_copy.wait()

    def project(t):
        for s in range(SUBS):
            share(t, s).wait_recv()
        behind = lax.rem(chip + n_chips - turn * t, n_chips) * 2 + core
        beyond = lax.rem(chip + n_chips + turn * t, n_chips) * 2 + 1 - core
        both = jnp.concatenate([mine[t], theirs[t]], axis=0)
        out = jnp.dot(both, wide[...], preferred_element_type=F32).astype(BF)
        next_ref[pl.ds(pl.multiple_of(behind * rows, rows), rows), :] = out[:rows]
        next_ref[pl.ds(pl.multiple_of(beyond * rows, rows), rows), :] = out[rows:]

    @pl.loop(1, n_chips - 1)
    def _(t):
        for s in range(SUBS):
            gather_on(t - 1, s).wait_recv()
            gather_on(t, s).start()
            share(t, s).start()
        project(t - 1)

    for s in range(SUBS):
        gather_on(n_chips - 2, s).wait_recv()
        share(n_chips - 1, s).start()
    project(n_chips - 2)

    weight_out.wait_send()
    weight_pair.wait_send()
    stream_out.wait_send()

    @pl.loop(1, n_seq)
    def _(i):
        exchange(lax.rem(me + i, n_seq)).wait_send()

    @pl.loop(0, n_chips)
    def _(t):
        for k in range(2):
            hand_on(t, k).wait_send()

    @pl.loop(0, n_chips - 1)
    def _(t):
        for s in range(SUBS):
            reduce_on(t, s).wait_send()
            gather_on(t, s).wait_send()
            share(t, s).wait_send()

    project(n_chips - 1)
    for s in range(SUBS):
        share(n_chips - 1, s).wait_send()


def local(projected, stream_before, out_weight, proj_weight, norm_gain, block_mask, token_order):
    n_seg, n_seq = lax.axis_size("segment"), lax.axis_size("seq")
    n_chips = n_seq // 2
    _, rows, width = stream_before.shape
    tokens = rows * n_seq
    head_cols = 3 * DH
    windows = tokens // WIN
    dma = pltpu.SemaphoreType.DMA
    any_space = pl.BlockSpec(memory_space=pl.ANY)
    vmem = pl.BlockSpec(memory_space=pltpu.VMEM)
    incoming, following = pl.pallas_call(
        functools.partial(kernel, n_seg, n_seq),
        out_shape=(
            jax.ShapeDtypeStruct((rows, width), BF),
            jax.ShapeDtypeStruct((tokens, head_cols), BF),
        ),
        in_specs=[
            vmem,
            pl.BlockSpec(memory_space=pltpu.SMEM),
            vmem,
            any_space,
            any_space,
            any_space,
            any_space,
        ],
        out_specs=(vmem, vmem),
        scratch_shapes=[
            pltpu.VMEM((n_seq, rows, head_cols), BF),
            pltpu.VMEM((tokens, tokens), BF),
            pltpu.VMEM((n_seq, rows, tokens), BF),
            pltpu.VMEM((windows, WIN, WIN), F32),
            pltpu.VMEM((tokens, DH), BF),
            pltpu.VMEM((n_chips, 2 * rows, DH), BF),
            pltpu.VMEM((2, n_chips, rows, DH), BF),
            pltpu.VMEM((2, DH, width), BF),
            pltpu.VMEM((rows, width), BF),
            pltpu.VMEM((width, head_cols), BF),
            pltpu.VMEM((rows, width), F32),
            pltpu.VMEM((n_chips - 1, rows, width), BF),
            pltpu.VMEM((n_chips - 1, rows, width), BF),
            pltpu.VMEM((n_chips, rows, width), BF),
            pltpu.VMEM((n_chips, rows, width), BF),
            dma, dma, dma((n_seq,)), dma((n_seq,)), dma, dma, dma, dma, dma, dma,
            dma((n_chips, 2)), dma((2, n_chips)),
            dma((n_chips - 1, SUBS)), dma((n_chips - 1, SUBS)),
            dma((n_chips - 1, SUBS)), dma((n_chips - 1, SUBS)),
            dma((n_chips, SUBS)), dma((n_chips, SUBS)),
        ],
        compiler_params=pltpu.CompilerParams(collective_id=0, has_side_effects=True),
        name="section_boundary",
    )(
        token_order.reshape(tokens // LANES, LANES),
        block_mask.reshape(-1),
        norm_gain,
        projected[0],
        stream_before[0],
        out_weight[0],
        proj_weight[0],
    )
    return (incoming[None], following[None])


def solution(mesh):
    placed = (
        P("segment", "seq", None),
        P("segment", "seq", None),
        P("segment", "seq", None),
        P("segment", None, "seq"),
        P("segment", None),
        P(),
        P(),
    )
    return jax.shard_map(
        local,
        mesh=mesh,
        in_specs=placed,
        out_specs=(P("segment", "seq", None), P("segment", None, "seq")),
        check_vma=False,
    )
```

time: 295 us -> 107 us (0.36)
  waiting for transfers between devices: 232 us -> 0 us
  Pallas kernels: 0 us -> 101 us
  starting transfers between devices: 17.2 us -> 0 us
  between operations: 14.2 us -> 0.64 us
  local copies, waits for them, and re-layouts: 16.9 us -> 5.13 us
  matrix products: 9.87 us -> 0 us
  other arithmetic: 4.81 us -> 0 us
    pallas_call x0 -> x1, Pallas kernels: none -> 101 us  [local(): pl.pallas_call(functools.partial(kernel, n_seg, n_seq), out_shape=(jax.Sh...]
    ppermute x1 -> x0, waiting for transfers between devices: 96.1 us -> none  [from_behind(): return lax.ppermute(x, axis, [(i, (i + by) % size) for i in range(size)])]
    reduce_scatter x1 -> x0, waiting for transfers between devices: 64 us -> none  [local(): lax.psum_scatter(jnp.dot(placed, out_weight[0], preferred_element_type=jn...]
    all_gather x1 -> x0, waiting for transfers between devices: 49 us -> none  [local(): assembled = lax.all_gather(stream_after, 'seq', axis=0, tiled=True)]
    all_to_all x1 -> x0, waiting for transfers between devices: 22.5 us -> none  [local(): lax.all_to_all(projected[0], 'seq', split_axis=1, concat_axis=0, tiled=True)]
    all_to_all x1 -> x0, starting transfers between devices: 13.9 us -> none  [local(): lax.all_to_all(projected[0], 'seq', split_axis=1, concat_axis=0, tiled=True)]
    dot_general x3 -> x0, matrix products: 9.36 us -> none  [the longest x1 5.45 us: local(): jnp.dot(normed, proj_weight[0], preferred_element_type=jnp.float32)]
    gather x2 -> x0, local copies, waits for them, and re-layouts: 8.87 us -> none  [local(): ordered = by_head.reshape(all_tokens, local_heads, 3, DH)[token_order]]
  transfers between devices with their start and end apart: 4 -> 0, of which waited for: 4 -> 0; matrix products, arithmetic and copies ran while one was open for 0% -> 0% of each run, Pallas kernels for 0% -> 0%
where the time goes in v1:
time: 107 us
  Pallas kernels  101 us (94%)
  local copies, waits for them, and re-layouts  5.13 us (5%)
    pallas_call x1, Pallas kernels, local(): pl.pallas_call(functools.partial(kernel, n_seg, n_seq), out_shape=(jax.Sh...  101 us
    unnamed x3, local copies, waits for them, and re-layouts  4.53 us

profile of v1, /device:TPU:1, one launch (start us, length us, event | category | flops | bytes accessed | tf_op | source)
XLA Modules:
  0.0 107.2 jit_solution(13633581377076830933)
XLA Ops:
  0.6 0.8 copy.10
  1.4 0.6 reshape.11.mask_ref
  2.0 101.5 %section_boundary.1 = (bf16[64,2048]{1,0:T(8,128)(2,1)}, bf16[1024,384]{1,0:T(8,128)(2,1)}) custom-call(s32[8,128]{1,0:T(8,128)} %bitcast.13, s32[16]{0:T(128)} %reshape.11.mask_ref, f32[1,2048]{1,0:T(1,128)} %gain_ref.1, bf16[64,6144]{1,0:T(8,128)(2,1)} %bitcast.9, bf16[64,2048]{1,0:T(8,128)(2,1)} %bitcast.12, bf16[128,2048]{1,0:T(8,128)(2,1)} %bitcast.10, ...), custom_call_target="tpu_custom_call" | custom-call | tf_op jit(solution)/shard_map/section_boundary/pallas_call | solution.py:288
  103.5 1.7 %copy.13 = bf16[1,64,2048]{2,1,0:T(8,128)(2,1)} copy(bf16[1,64,2048]{2,1,0:T(8,128)(2,1)} %bitcast.11) | data formatting | bytes 524288
  105.1 2.1 %copy.14 = bf16[1,1024,384]{2,1,0:T(8,128)(2,1)} copy(bf16[1,1024,384]{2,1,0:T(8,128)(2,1)} %bitcast.8) | data formatting | bytes 1572864

commit v2 on v1

--- a/solution.py
+++ b/solution.py
@@ -34,7 +34,7 @@
     order_ref, mask_ref, gain_ref, projected, stream_before, out_weight, proj_weight,
     incoming_ref, next_ref,
     qkv, perm, unperm, bias, att, placed, gathered, weight, stream, wide, total,
-    rs_out, rs_in, mine, theirs,
+    rs_out, rs_in, mine, theirs, landed,
     own_sem, pw_sem, qkv_send, qkv_recv, w_send, w_recv, wp_send, wp_recv, st_send, st_recv,
     att_send, att_recv, rs_send, rs_recv, ag_send, ag_recv, pr_send, pr_recv,
 ):
@@ -46,7 +46,12 @@
     seg, me = lax.axis_index("segment"), lax.axis_index("seq")
     core, chip = lax.rem(me, 2), me // 2
     turn = 1 - 2 * core
-    ahead = {"seq": lax.rem(chip + turn + n_chips, n_chips) * 2 + core}
+    half = n_chips // 2
+
+    def toward(t):
+        way = turn * (1 - 2 * lax.rem(t, 2))
+        return {"seq": lax.rem(chip + n_chips + way, n_chips) * 2 + core}
+
     peer = {"seq": chip * 2 + 1 - core}
     seg_next, seg_last = lax.rem(seg + 1, n_seg), lax.rem(seg + n_seg - 1, n_seg)
 
@@ -76,8 +81,8 @@
     def exchange(j):
         return remote(block_of(j), qkv.at[me], qkv_send.at[j], qkv_recv.at[me], {"seq": j})
 
-    steps = [n_chips // 2]
-    for d in range(n_chips // 2 - 1, 0, -1):
+    steps = [half]
+    for d in range(half - 1, 0, -1):
         steps += [d, n_chips - d]
     for d in steps:
         for k in range(2):
@@ -111,13 +116,12 @@
                 here == there, 1.0, 0.0
             ).astype(BF)
 
-    for w in range(tokens // WIN):
-        for a in range(WIN // BLOCK):
-            for b in range(WIN // BLOCK):
-                seen = mask_ref[(w * (WIN // BLOCK) + a) * (WIN // BLOCK) + b]
-                level = (1 - jnp.minimum(seen, 1)).astype(F32) * HIDDEN
+    for a in range(WIN // BLOCK):
+        for b in range(WIN // BLOCK):
+            level = jnp.where(mask_ref[a, b : b + 1, :] > 0, 0.0, HIDDEN)
+            for w in range(tokens // WIN):
                 bias[w, a * BLOCK : (a + 1) * BLOCK, b * BLOCK : (b + 1) * BLOCK] = (
-                    jnp.zeros((BLOCK, BLOCK), F32) + level
+                    jnp.broadcast_to(level[:, w : w + 1], (BLOCK, BLOCK))
                 )
 
     weight_out.wait_recv()
@@ -154,8 +158,10 @@
 
     @pl.loop(0, n_chips)
     def _(t):
-        up = lax.rem(chip + 2 * n_chips - 1 - t, n_chips)
-        down = lax.rem(chip + 1 + t, n_chips)
+        odd = lax.rem(t, 2)
+        off = (1 - 2 * odd) * (half - odd - t // 2)
+        up = lax.rem(chip + n_chips + off, n_chips)
+        down = lax.rem(chip + n_chips - off, n_chips)
         both = jnp.concatenate([unperm[up], unperm[n_chips + down]], axis=0)
         placed[t] = jnp.dot(both, att[...], preferred_element_type=F32).astype(BF)
         for k in range(2):
@@ -166,7 +172,7 @@
     )
     other_weight.wait_recv()
 
-    def term(t):
+    def term(t, at):
         for k in range(2):
             remote(
                 gathered.at[k, t], gathered.at[k, t], att_send.at[t, k], att_recv.at[k, t], peer
@@ -174,81 +180,119 @@
         left = jnp.concatenate([gathered[0, t], gathered[1, t]], axis=1)
         for n in range(width // COLS):
             cut = slice(n * COLS, (n + 1) * COLS)
-            total[:, cut] = jnp.dot(
+            total[at, :, cut] = jnp.dot(
                 left, weight[:, :, cut].reshape(2 * DH, COLS), preferred_element_type=F32
             )
 
     def reduce_on(t, s):
         cut = pl.ds(s * part, part)
         return remote(
-            rs_out.at[t, cut], rs_in.at[t, cut], rs_send.at[t, s], rs_recv.at[t, s], ahead
-        )
-
-    term(0)
+            rs_out.at[t, cut], rs_in.at[t, cut], rs_send.at[t, s], rs_recv.at[t, s], toward(t)
+        )
+
+    def pass_on(t, at, s, first):
+        cut = pl.ds(s * part, part)
+        value = total[at, cut, :]
+        if not first:
+            reduce_on(t - 2, s).wait_recv()
+            value += rs_in[t - 2, cut, :].astype(F32)
+        rs_out[t, cut, :] = value.astype(BF)
+        reduce_on(t, s).start()
+
+    for t in range(2):
+        term(t, t)
+        for s in range(SUBS):
+            pass_on(t, t, s, True)
+
+    @pl.loop(1, half - 1)
+    def _(p):
+        for t in range(2):
+            term(2 * p + t, t)
+        for s in range(SUBS):
+            for t in range(2):
+                pass_on(2 * p + t, t, s, False)
+
+    for t in range(2):
+        term(n_chips - 2 + t, t)
     for s in range(SUBS):
+        pass_on(n_chips - 2, 0, s, False)
+
+    def gather_on(u, s):
         cut = pl.ds(s * part, part)
-        rs_out[0, cut, :] = total[cut, :].astype(BF)
-        reduce_on(0, s).start()
-
-    @pl.loop(1, n_chips - 1)
-    def _(t):
-        term(t)
-        for s in range(SUBS):
-            cut = pl.ds(s * part, part)
-            reduce_on(t - 1, s).wait_recv()
-            rs_out[t, cut, :] = (total[cut, :] + rs_in[t - 1, cut, :].astype(F32)).astype(BF)
-            reduce_on(t, s).start()
-
-    def gather_on(t, s):
+        slot = max(u - 1, 0) if isinstance(u, int) else jnp.maximum(u - 1, 0)
+        return remote(
+            mine.at[slot, cut], mine.at[u + 1, cut], ag_send.at[u, s], ag_recv.at[u, s], toward(u)
+        )
+
+    def share(v, s):
         cut = pl.ds(s * part, part)
         return remote(
-            mine.at[t, cut], mine.at[t + 1, cut], ag_send.at[t, s], ag_recv.at[t, s], ahead
-        )
-
-    def share(t, s):
-        cut = pl.ds(s * part, part)
-        return remote(
-            mine.at[t, cut], theirs.at[t, cut], pr_send.at[t, s], pr_recv.at[t, s], peer
-        )
-
-    term(n_chips - 1)
+            mine.at[v, cut], theirs.at[v, cut], pr_send.at[v, s], pr_recv.at[v, s], peer
+        )
+
     stream_out.wait_recv()
     for s in range(SUBS):
         cut = pl.ds(s * part, part)
-        reduce_on(n_chips - 2, s).wait_recv()
-        branch = total[cut, :] + rs_in[n_chips - 2, cut, :].astype(F32)
+        branch = total[1, cut, :]
+        for t in (n_chips - 3, n_chips - 2):
+            reduce_on(t, s).wait_recv()
+            branch += rs_in[t, cut, :].astype(F32)
         after = (stream[cut, :].astype(F32) + branch).astype(BF)
         incoming_ref[cut, :] = after
         widened = after.astype(F32)
         scale = lax.rsqrt(jnp.mean(widened * widened, axis=-1, keepdims=True) + 1e-06)
         mine[0, cut, :] = (widened * scale * gain_ref[...]).astype(BF)
-        gather_on(0, s).start()
+        for u in range(2):
+            gather_on(u, s).start()
         share(0, s).start()
 
     wide_copy.wait()
 
-    def project(t):
+    def place(v, ring, out):
+        way = turn * (2 * lax.rem(v, 2) - 1) * (1 - 2 * ring)
+        at = lax.rem(chip + n_chips - way * ((v + 1) // 2), n_chips) * 2
+        at += core if ring == 0 else 1 - core
+        next_ref[pl.ds(pl.multiple_of(at * rows, rows), rows), :] = out.astype(BF)
+
+    def piece(slots, n):
+        cut = slice(n * (width // SUBS), (n + 1) * (width // SUBS))
+        blocks = [buffer[v, :, cut] for v in slots for buffer in (mine, theirs)]
+        out = jnp.dot(
+            jnp.concatenate(blocks, axis=0), wide[cut, :], preferred_element_type=F32
+        )
+        span = slice(0, len(blocks) * rows)
+        if n > 0:
+            out += landed[span, :]
+        if n < SUBS - 1:
+            landed[span, :] = out
+        else:
+            for i, v in enumerate(slots):
+                for ring in range(2):
+                    at = (2 * i + ring) * rows
+                    place(v, ring, out[at : at + rows])
+
+    def arrived(slots):
+        for v in slots:
+            for s in range(SUBS):
+                share(v, s).wait_recv()
+
+    def round_of(a, final):
+        sends = [2 * a, 2 * a + 1]
+        slots = [2 * a - 1, 2 * a] if a > 0 else [0]
         for s in range(SUBS):
-            share(t, s).wait_recv()
-        behind = lax.rem(chip + n_chips - turn * t, n_chips) * 2 + core
-        beyond = lax.rem(chip + n_chips + turn * t, n_chips) * 2 + 1 - core
-        both = jnp.concatenate([mine[t], theirs[t]], axis=0)
-        out = jnp.dot(both, wide[...], preferred_element_type=F32).astype(BF)
-        next_ref[pl.ds(pl.multiple_of(behind * rows, rows), rows), :] = out[:rows]
-        next_ref[pl.ds(pl.multiple_of(beyond * rows, rows), rows), :] = out[rows:]
-
-    @pl.loop(1, n_chips - 1)
-    def _(t):
-        for s in range(SUBS):
-            gather_on(t - 1, s).wait_recv()
-            gather_on(t, s).start()
-            share(t, s).start()
-        project(t - 1)
-
-    for s in range(SUBS):
-        gather_on(n_chips - 2, s).wait_recv()
-        share(n_chips - 1, s).start()
-    project(n_chips - 2)
+            for u in sends[: 1 if final else 2]:
+                gather_on(u, s).wait_recv()
+                if u + 2 < n_chips - 1:
+                    gather_on(u + 2, s).start()
+                share(u + 1, s).start()
+            if s == 1:
+                arrived(slots)
+            if s > 0:
+                piece(slots, s - 1)
+        piece(slots, SUBS - 1)
+
+    for a in range(half):
+        round_of(a, a == half - 1)
 
     weight_out.wait_send()
     weight_pair.wait_send()
@@ -270,9 +314,12 @@
             gather_on(t, s).wait_send()
             share(t, s).wait_send()
 
-    project(n_chips - 1)
+    last = n_chips - 1
+    place(last, 0, jnp.dot(mine[last], wide[...], preferred_element_type=F32))
+    arrived([last])
+    place(last, 1, jnp.dot(theirs[last], wide[...], preferred_element_type=F32))
     for s in range(SUBS):
-        share(n_chips - 1, s).wait_send()
+        share(last, s).wait_send()
 
 
 def local(projected, stream_before, out_weight, proj_weight, norm_gain, block_mask, token_order):
@@ -288,12 +335,12 @@
     incoming, following = pl.pallas_call(
         functools.partial(kernel, n_seg, n_seq),
         out_shape=(
-            jax.ShapeDtypeStruct((rows, width), BF),
-            jax.ShapeDtypeStruct((tokens, head_cols), BF),
+            pltpu.VMEM((rows, width), BF),
+            pltpu.VMEM((tokens, head_cols), BF),
         ),
         in_specs=[
             vmem,
-            pl.BlockSpec(memory_space=pltpu.SMEM),
+            vmem,
             vmem,
             any_space,
             any_space,
@@ -312,11 +359,12 @@
             pltpu.VMEM((2, DH, width), BF),
             pltpu.VMEM((rows, width), BF),
             pltpu.VMEM((width, head_cols), BF),
-            pltpu.VMEM((rows, width), F32),
+            pltpu.VMEM((2, rows, width), F32),
             pltpu.VMEM((n_chips - 1, rows, width), BF),
             pltpu.VMEM((n_chips - 1, rows, width), BF),
             pltpu.VMEM((n_chips, rows, width), BF),
             pltpu.VMEM((n_chips, rows, width), BF),
+            pltpu.VMEM((4 * rows, head_cols), F32),
             dma, dma, dma((n_seq,)), dma((n_seq,)), dma, dma, dma, dma, dma, dma,
             dma((n_chips, 2)), dma((2, n_chips)),
             dma((n_chips - 1, SUBS)), dma((n_chips - 1, SUBS)),
@@ -327,7 +375,7 @@
         name="section_boundary",
     )(
         token_order.reshape(tokens // LANES, LANES),
-        block_mask.reshape(-1),
+        block_mask.transpose(1, 2, 0),
         norm_gain,
         projected[0],
         stream_before[0],

time: 107 us -> 96.6 us (0.903)
  Pallas kernels: 101 us -> 94.2 us
  local copies, waits for them, and re-layouts: 5.13 us -> 1.58 us
    pallas_call x1, Pallas kernels: 101 us -> 94.2 us  [local(): pl.pallas_call(functools.partial(kernel, n_seg, n_seq), out_shape=(pltpu....]
    unnamed x3 -> x2, local copies, waits for them, and re-layouts: 4.53 us -> 1.58 us
where the time goes in v2:
time: 96.6 us; the launch traced here: 96.4 us
  Pallas kernels  94.2 us (98%)
  local copies, waits for them, and re-layouts  1.58 us (2%)
    pallas_call x1, Pallas kernels, local(): pl.pallas_call(functools.partial(kernel, n_seg, n_seq), out_shape=(pltpu....  94.2 us

profile of v2, /device:TPU:1, one launch (start us, length us, event | category | flops | bytes accessed | tf_op | source)
XLA Modules:
  0.0 96.4 jit_solution(11815238132719794619)
XLA Ops:
  0.6 94.2 %section_boundary.1 = (bf16[64,2048]{1,0:T(8,128)(2,1)S(1)}, bf16[1024,384]{1,0:T(8,128)(2,1)S(1)}) custom-call(s32[8,128]{1,0:T(8,128)} %bitcast.14, s32[2,2,4]{2,1,0:T(2,128)} %bitcast.15, f32[1,2048]{1,0:T(1,128)} %gain_ref.1, bf16[64,6144]{1,0:T(8,128)(2,1)} %bitcast.11, bf16[64,2048]{1,0:T(8,128)(2,1)} %bitcast.13, bf16[128,2048]{1,0:T(8,128)(2,1)} %bitcast.12, ...), custom_call_target="tpu_custom_call" | custom-call | tf_op jit(solution)/shard_map/section_boundary/pallas_call | solution.py:335
  94.8 0.7 copy.11
  95.5 0.9 copy.12

commit v3 on v2

--- a/solution.py
+++ b/solution.py
@@ -31,11 +31,11 @@
 
 def kernel(
     n_seg, n_seq,
-    order_ref, mask_ref, gain_ref, projected, stream_before, out_weight, proj_weight,
+    order_in, mask_in, gain_in, projected, stream_before, out_weight, proj_weight,
     incoming_ref, next_ref,
-    qkv, perm, unperm, bias, att, placed, gathered, weight, stream, wide, total,
+    order_ref, mask_ref, gain_ref, pair, value, belongs, member, seen, bias, probs, placed, gathered, weight, stream, wide, total,
     rs_out, rs_in, mine, theirs, landed,
-    own_sem, pw_sem, qkv_send, qkv_recv, w_send, w_recv, wp_send, wp_recv, st_send, st_recv,
+    small_sem, own_sem, pw_sem, qkv_send, qkv_recv, w_send, w_recv, wp_send, wp_recv, st_send, st_recv,
     att_send, att_recv, rs_send, rs_recv, ag_send, ag_recv, pr_send, pr_recv,
 ):
     n_chips = n_seq // 2
@@ -55,99 +55,140 @@
     peer = {"seq": chip * 2 + 1 - core}
     seg_next, seg_last = lax.rem(seg + 1, n_seg), lax.rem(seg + n_seg - 1, n_seg)
 
+    hops = [half]
+    for d in range(half - 1, 0, -1):
+        hops += [d, n_chips - d]
+
     barrier = pltpu.get_barrier_semaphore()
-    for i in range(1, n_seq):
+
+    def greet(device):
         pl.semaphore_signal(
-            barrier, inc=1, device_id={"seq": lax.rem(me + i, n_seq)},
-            device_id_type=pl.DeviceIdType.MESH,
-        )
+            barrier, inc=1, device_id=device, device_id_type=pl.DeviceIdType.MESH
+        )
+
+    for d in hops:
+        for k in range(2):
+            greet({"seq": lax.rem(chip + d, n_chips) * 2 + k})
+    greet(peer)
     for other in (seg_next, seg_last):
         for k in range(2):
-            pl.semaphore_signal(
-                barrier, inc=1, device_id={"segment": other, "seq": chip * 2 + k},
-                device_id_type=pl.DeviceIdType.MESH,
-            )
-
-    def block_of(j):
-        return projected.at[:, pl.ds(pl.multiple_of(j * head_cols, LANES), head_cols)]
-
-    own = pltpu.make_async_copy(block_of(me), qkv.at[me], own_sem)
-    own.start()
+            greet({"segment": other, "seq": chip * 2 + k})
+
+    def block_of(j, n):
+        at = j * head_cols + n * 2 * DH
+        return projected.at[:, pl.ds(pl.multiple_of(at, LANES), (2 - n) * DH)]
+
+    small = [
+        pltpu.make_async_copy(there, here, small_sem.at[n])
+        for n, (there, here) in enumerate(
+            ((order_in, order_ref), (mask_in, mask_ref), (gain_in, gain_ref))
+        )
+    ]
+    for copy in small:
+        copy.start()
+    own = [
+        pltpu.make_async_copy(block_of(me, n), (pair, value)[n].at[me], own_sem.at[n])
+        for n in range(2)
+    ]
+    for n in range(2):
+        own[n].start()
     wide_copy = pltpu.make_async_copy(proj_weight, wide, pw_sem)
     wide_copy.start()
 
     pl.semaphore_wait(barrier, n_seq + 3)
 
-    def exchange(j):
-        return remote(block_of(j), qkv.at[me], qkv_send.at[j], qkv_recv.at[me], {"seq": j})
-
-    steps = [half]
-    for d in range(half - 1, 0, -1):
-        steps += [d, n_chips - d]
-    for d in steps:
-        for k in range(2):
-            exchange(lax.rem(chip + d, n_chips) * 2 + k).start()
-    exchange(chip * 2 + 1 - core).start()
+    def exchange(j, n):
+        return remote(
+            block_of(j, n), (pair, value)[n].at[me], qkv_send.at[n, j], qkv_recv.at[n, me],
+            {"seq": j},
+        )
+
+    def from_all(n):
+        own[n].wait()
+
+        @pl.loop(1, n_seq)
+        def _(i):
+            j = lax.rem(me + i, n_seq)
+            there = (pair, value)[n].at[j]
+            remote(there, there, qkv_send.at[n, j], qkv_recv.at[n, j], {"seq": j}).wait_recv()
+
+    def to_all(n):
+        for d in hops:
+            for k in range(2):
+                exchange(lax.rem(chip + d, n_chips) * 2 + k, n).start()
+        exchange(chip * 2 + 1 - core, n).start()
+
+    to_all(0)
     straight = {"segment": seg_next, "seq": me}
     weight_out = remote(out_weight, weight.at[core], w_send, w_recv, straight)
     weight_out.start()
+    to_all(1)
     stream_out = remote(stream_before, stream, st_send, st_recv, straight)
     stream_out.start()
 
     tiles = tokens // LANES
+    for copy in small:
+        copy.wait()
     order = order_ref[...]
-
-    for q in range(tiles):
-        spread = jnp.broadcast_to(order[q : q + 1, :], (LANES, LANES)).astype(F32)
-        column = jnp.transpose(spread)
-        for r in range(tiles):
-            there = lax.broadcasted_iota(jnp.int32, (LANES, LANES), 1) + r * LANES
-            perm[q * LANES : (q + 1) * LANES, r * LANES : (r + 1) * LANES] = jnp.where(
-                column == there.astype(F32), 1.0, 0.0
-            ).astype(BF)
 
     @pl.loop(0, n_seq)
     def _(b):
-        base = lax.rem(b, n_chips) * (2 * rows) + (b // n_chips) * rows
-        there = lax.broadcasted_iota(jnp.int32, (rows, LANES), 0) + base
+        there = lax.broadcasted_iota(jnp.int32, (rows, LANES), 0) + b * rows
         for q in range(tiles):
             here = jnp.broadcast_to(order[q : q + 1, :], (rows, LANES))
-            unperm[b, :, q * LANES : (q + 1) * LANES] = jnp.where(
-                here == there, 1.0, 0.0
-            ).astype(BF)
-
-    for a in range(WIN // BLOCK):
-        for b in range(WIN // BLOCK):
-            level = jnp.where(mask_ref[a, b : b + 1, :] > 0, 0.0, HIDDEN)
+            belongs[pl.ds(pl.multiple_of(b * rows, rows), rows), q * LANES : (q + 1) * LANES] = (
+                jnp.where(here == there, 1.0, 0.0).astype(BF)
+            )
+
+    place_block = lax.shift_right_logical(lax.broadcasted_iota(jnp.int32, (tokens, LANES), 0), 7)
+    lane = lax.broadcasted_iota(jnp.int32, (tokens, LANES), 1)
+    in_block = jnp.where(place_block == lane, 1.0, 0.0).astype(BF)
+    member[...] = jnp.dot(belongs[...], in_block, preferred_element_type=F32).astype(BF)
+
+    down = lax.broadcasted_iota(jnp.int32, (LANES, LANES), 0)
+    across = lax.broadcasted_iota(jnp.int32, (LANES, LANES), 1)
+    sees = jnp.zeros((LANES, LANES), F32)
+    per = WIN // BLOCK
+    for a in range(per):
+        for b in range(per):
+            open_ = jnp.where(mask_ref[a, b : b + 1, :] > 0, 1.0, 0.0)
             for w in range(tokens // WIN):
-                bias[w, a * BLOCK : (a + 1) * BLOCK, b * BLOCK : (b + 1) * BLOCK] = (
-                    jnp.broadcast_to(level[:, w : w + 1], (BLOCK, BLOCK))
-                )
+                here = (down == w * per + a) & (across == w * per + b)
+                level = jnp.broadcast_to(open_[:, w : w + 1], (LANES, LANES))
+                sees += jnp.where(here, level, 0.0)
+    seen[...] = jnp.dot(
+        member[...], sees.astype(BF), preferred_element_type=F32
+    ).astype(BF)
+
+    @pl.loop(0, tiles)
+    def _(r):
+        cut = pl.ds(pl.multiple_of(r * LANES, LANES), LANES)
+        allowed = lax.dot_general(
+            seen[cut, :], member[...], (((1,), (1,)), ((), ())), preferred_element_type=F32
+        )
+        bias[cut, :] = (1.0 - allowed) * HIDDEN
+
+    from_all(0)
+    each = LANES // rows
+
+    @pl.loop(0, tiles)
+    def _(r):
+        cut = pl.ds(pl.multiple_of(r * LANES, LANES), LANES)
+        query = pair[pl.ds(r * each, each), :, :DH].reshape(LANES, DH)
+        key = pair[:, :, DH:].reshape(tokens, DH)
+        scores = lax.dot_general(
+            query, key, (((1,), (1,)), ((), ())), preferred_element_type=F32
+        )
+        scores = scores * DH ** (-0.5) + bias[cut, :]
+        highest = jnp.max(scores, axis=-1, keepdims=True)
+        raised = jnp.exp(scores - highest)
+        shares = raised * (1.0 / jnp.sum(raised, axis=-1, keepdims=True))
+        probs[pl.ds(r * each, each)] = shares.astype(BF).reshape(each, rows, tokens)
 
     weight_out.wait_recv()
     weight_pair = remote(weight.at[core], weight.at[core], wp_send, wp_recv, peer)
     weight_pair.start()
-    own.wait()
-
-    @pl.loop(1, n_seq)
-    def _(i):
-        j = lax.rem(me + i, n_seq)
-        remote(qkv.at[j], qkv.at[j], qkv_send.at[j], qkv_recv.at[j], {"seq": j}).wait_recv()
-
-    for w in range(tokens // WIN):
-        seen = slice(w * WIN, (w + 1) * WIN)
-        picked = jnp.dot(
-            perm[seen, :], qkv[...].reshape(tokens, head_cols), preferred_element_type=F32
-        ).astype(BF)
-        scores = lax.dot_general(
-            picked[:, :DH], picked[:, DH : 2 * DH], (((1,), (1,)), ((), ())),
-            preferred_element_type=F32,
-        )
-        scores = scores * DH ** (-0.5) + bias[w]
-        highest = jnp.max(scores, axis=-1, keepdims=True)
-        raised = jnp.exp(scores - highest)
-        probs = (raised / jnp.sum(raised, axis=-1, keepdims=True)).astype(BF)
-        att[seen, :] = jnp.dot(probs, picked[:, 2 * DH :], preferred_element_type=F32).astype(BF)
+    from_all(1)
 
     def hand_on(t, k):
         return remote(
@@ -162,8 +203,10 @@
         off = (1 - 2 * odd) * (half - odd - t // 2)
         up = lax.rem(chip + n_chips + off, n_chips)
         down = lax.rem(chip + n_chips - off, n_chips)
-        both = jnp.concatenate([unperm[up], unperm[n_chips + down]], axis=0)
-        placed[t] = jnp.dot(both, att[...], preferred_element_type=F32).astype(BF)
+        both = jnp.concatenate([probs[up * 2], probs[down * 2 + 1]], axis=0)
+        placed[t] = jnp.dot(
+            both, value[...].reshape(tokens, DH), preferred_element_type=F32
+        ).astype(BF)
         for k in range(2):
             hand_on(t, k).start()
 
@@ -300,7 +343,8 @@
 
     @pl.loop(1, n_seq)
     def _(i):
-        exchange(lax.rem(me + i, n_seq)).wait_send()
+        for n in range(2):
+            exchange(lax.rem(me + i, n_seq), n).wait_send()
 
     @pl.loop(0, n_chips)
     def _(t):
@@ -322,13 +366,25 @@
         share(last, s).wait_send()
 
 
+def write_out(incoming, following, incoming_out, following_out, sem):
+    copies = [
+        pltpu.make_async_copy(here, there, sem.at[n])
+        for n, (here, there) in enumerate(
+            ((incoming, incoming_out), (following, following_out))
+        )
+    ]
+    for copy in copies:
+        copy.start()
+    for copy in copies:
+        copy.wait()
+
+
 def local(projected, stream_before, out_weight, proj_weight, norm_gain, block_mask, token_order):
     n_seg, n_seq = lax.axis_size("segment"), lax.axis_size("seq")
     n_chips = n_seq // 2
     _, rows, width = stream_before.shape
     tokens = rows * n_seq
     head_cols = 3 * DH
-    windows = tokens // WIN
     dma = pltpu.SemaphoreType.DMA
     any_space = pl.BlockSpec(memory_space=pl.ANY)
     vmem = pl.BlockSpec(memory_space=pltpu.VMEM)
@@ -339,9 +395,9 @@
             pltpu.VMEM((tokens, head_cols), BF),
         ),
         in_specs=[
-            vmem,
-            vmem,
-            vmem,
+            any_space,
+            any_space,
+            any_space,
             any_space,
             any_space,
             any_space,
@@ -349,11 +405,16 @@
         ],
         out_specs=(vmem, vmem),
         scratch_shapes=[
-            pltpu.VMEM((n_seq, rows, head_cols), BF),
+            pltpu.VMEM((tokens // LANES, LANES), jnp.int32),
+            pltpu.VMEM((WIN // BLOCK, WIN // BLOCK, tokens // WIN), jnp.int32),
+            pltpu.VMEM((1, width), F32),
+            pltpu.VMEM((n_seq, rows, 2 * DH), BF),
+            pltpu.VMEM((n_seq, rows, DH), BF),
             pltpu.VMEM((tokens, tokens), BF),
+            pltpu.VMEM((tokens, LANES), BF),
+            pltpu.VMEM((tokens, LANES), BF),
+            pltpu.VMEM((tokens, tokens), F32),
             pltpu.VMEM((n_seq, rows, tokens), BF),
-            pltpu.VMEM((windows, WIN, WIN), F32),
-            pltpu.VMEM((tokens, DH), BF),
             pltpu.VMEM((n_chips, 2 * rows, DH), BF),
             pltpu.VMEM((2, n_chips, rows, DH), BF),
             pltpu.VMEM((2, DH, width), BF),
@@ -365,7 +426,7 @@
             pltpu.VMEM((n_chips, rows, width), BF),
             pltpu.VMEM((n_chips, rows, width), BF),
             pltpu.VMEM((4 * rows, head_cols), F32),
-            dma, dma, dma((n_seq,)), dma((n_seq,)), dma, dma, dma, dma, dma, dma,
+            dma((3,)), dma((2,)), dma, dma((2, n_seq)), dma((2, n_seq)), dma, dma, dma, dma, dma, dma,
             dma((n_chips, 2)), dma((2, n_chips)),
             dma((n_chips - 1, SUBS)), dma((n_chips - 1, SUBS)),
             dma((n_chips - 1, SUBS)), dma((n_chips - 1, SUBS)),
@@ -382,6 +443,17 @@
         out_weight[0],
         proj_weight[0],
     )
+    incoming, following = pl.pallas_call(
+        write_out,
+        out_shape=(
+            jax.ShapeDtypeStruct((rows, width), BF),
+            jax.ShapeDtypeStruct((tokens, head_cols), BF),
+        ),
+        in_specs=[vmem, vmem],
+        out_specs=(any_space, any_space),
+        scratch_shapes=[dma((2,))],
+        name="write_out",
+    )(*(pltpu.with_memory_space_constraint(x, pltpu.VMEM) for x in (incoming, following)))
     return (incoming[None], following[None])
 
 

time: 96.6 us -> 93.9 us (0.972)
  local copies, waits for them, and re-layouts: 1.58 us -> 0 us
  Pallas kernels: 94.2 us -> 93.2 us
    pallas_call x1, Pallas kernels: 94.2 us -> 92.2 us  [local(): pl.pallas_call(functools.partial(kernel, n_seg, n_seq), out_shape=(pltpu....]
    unnamed x2 -> x0, local copies, waits for them, and re-layouts: 1.58 us -> none
    pallas_call x0 -> x1, Pallas kernels: none -> 0.99 us  [local(): pl.pallas_call(write_out, out_shape=(jax.ShapeDtypeStruct((rows, width),...]
where the time goes in v3:
time: 93.9 us; the launch traced here: 93.8 us
  Pallas kernels  93.2 us (99%)
    pallas_call x1, Pallas kernels, local(): pl.pallas_call(functools.partial(kernel, n_seg, n_seq), out_shape=(pltpu....  92.2 us

profile of v3, /device:TPU:1, one launch (start us, length us, event | category | flops | bytes accessed | tf_op | source)
XLA Modules:
  0.0 93.8 jit_solution(9801111499143626124)
XLA Ops:
  0.6 92.2 %section_boundary.1 = (bf16[64,2048]{1,0:T(8,128)(2,1)S(1)}, bf16[1024,384]{1,0:T(8,128)(2,1)S(1)}) custom-call(s32[8,128]{1,0:T(8,128)} %bitcast.12, s32[2,2,4]{2,1,0:T(2,128)} %bitcast.13, f32[1,2048]{1,0:T(1,128)} %gain_in.1, bf16[64,6144]{1,0:T(8,128)(2,1)} %bitcast.9, bf16[64,2048]{1,0:T(8,128)(2,1)} %bitcast.11, bf16[128,2048]{1,0:T(8,128)(2,1)} %bitcast.10, ...), custom_call_target="tpu_custom_call" | custom-call | tf_op jit(solution)/shard_map/section_boundary/pallas_call | solution.py:391
  92.8 1.0 %write_out.1 = (bf16[64,2048]{1,0:T(8,128)(2,1)}, bf16[1024,384]{1,0:T(8,128)(2,1)}) custom-call(bf16[64,2048]{1,0:T(8,128)(2,1)S(1)} %get-tuple-element.6.incoming, bf16[1024,384]{1,0:T(8,128)(2,1)S(1)} %get-tuple-element.7.following), custom_call_target="tpu_custom_call" | custom-call | tf_op jit(solution)/shard_map/write_out/pallas_call | solution.py:446

commit v4 on v3

--- a/solution.py
+++ b/solution.py
@@ -12,6 +12,7 @@
 BLOCK = 128
 LANES = 128
 SUBS = 4
+LATE = 0
 COLS = 512
 HIDDEN = -1e30
 BF = jnp.bfloat16
@@ -33,10 +34,11 @@
     n_seg, n_seq,
     order_in, mask_in, gain_in, projected, stream_before, out_weight, proj_weight,
     incoming_ref, next_ref,
-    order_ref, mask_ref, gain_ref, pair, value, belongs, member, seen, bias, probs, placed, gathered, weight, stream, wide, total,
-    rs_out, rs_in, mine, theirs, landed,
-    small_sem, own_sem, pw_sem, qkv_send, qkv_recv, w_send, w_recv, wp_send, wp_recv, st_send, st_recv,
-    att_send, att_recv, rs_send, rs_recv, ag_send, ag_recv, pr_send, pr_recv,
+    order_ref, mask_ref, gain_ref, pair, value, belongs, member, seen, bias, probs, placed,
+    beside, gathered, near, far, stream, wide, total, rs_out, rs_in, ready, early, mine, theirs, landed,
+    small_sem, own_sem, pw_sem, qkv_send, qkv_recv,
+    w_sem, near_send, near_recv, far_send, far_recv, st_send, st_recv,
+    by_send, by_recv, att_send, att_recv, early_send, early_recv, rs_send, rs_recv, ag_send, ag_recv, pr_send, pr_recv,
 ):
     n_chips = n_seq // 2
     rows, width = stream.shape
@@ -47,6 +49,7 @@
     core, chip = lax.rem(me, 2), me // 2
     turn = 1 - 2 * core
     half = n_chips // 2
+    mid = width // 2
 
     def toward(t):
         way = turn * (1 - 2 * lax.rem(t, 2))
@@ -70,9 +73,8 @@
         for k in range(2):
             greet({"seq": lax.rem(chip + d, n_chips) * 2 + k})
     greet(peer)
-    for other in (seg_next, seg_last):
-        for k in range(2):
-            greet({"segment": other, "seq": chip * 2 + k})
+    for k in range(2):
+        greet({"segment": seg_last, "seq": chip * 2 + k})
 
     def block_of(j, n):
         at = j * head_cols + n * 2 * DH
@@ -95,7 +97,7 @@
     wide_copy = pltpu.make_async_copy(proj_weight, wide, pw_sem)
     wide_copy.start()
 
-    pl.semaphore_wait(barrier, n_seq + 3)
+    pl.semaphore_wait(barrier, n_seq + 1)
 
     def exchange(j, n):
         return remote(
@@ -120,8 +122,23 @@
 
     to_all(0)
     straight = {"segment": seg_next, "seq": me}
-    weight_out = remote(out_weight, weight.at[core], w_send, w_recv, straight)
-    weight_out.start()
+    columns = [out_weight.at[:, pl.ds(q * mid, mid)] for q in range(2)]
+    kept = pltpu.make_async_copy(columns[0], near.at[0], w_sem)
+    kept.start()
+    near_out = remote(columns[0], near.at[1], near_send, near_recv, peer)
+    near_out.start()
+
+    def far_out(k):
+        return remote(
+            columns[1], far.at[core], far_send.at[k], far_recv.at[core],
+            {"segment": seg_next, "seq": chip * 2 + k},
+        )
+
+    def far_in(k):
+        return remote(far.at[k], far.at[k], far_send.at[k], far_recv.at[k], peer)
+
+    for k in range(2):
+        far_out(k).start()
     to_all(1)
     stream_out = remote(stream_before, stream, st_send, st_recv, straight)
     stream_out.start()
@@ -185,10 +202,11 @@
         shares = raised * (1.0 / jnp.sum(raised, axis=-1, keepdims=True))
         probs[pl.ds(r * each, each)] = shares.astype(BF).reshape(each, rows, tokens)
 
-    weight_out.wait_recv()
-    weight_pair = remote(weight.at[core], weight.at[core], wp_send, wp_recv, peer)
-    weight_pair.start()
     from_all(1)
+
+    def hand_over(t):
+        other = pl.ds(pl.multiple_of((1 - core) * rows, rows), rows)
+        return remote(placed.at[t, other], beside.at[t], by_send.at[t], by_recv.at[t], peer)
 
     def hand_on(t, k):
         return remote(
@@ -207,58 +225,96 @@
         placed[t] = jnp.dot(
             both, value[...].reshape(tokens, DH), preferred_element_type=F32
         ).astype(BF)
+        hand_over(t).start()
         for k in range(2):
             hand_on(t, k).start()
 
-    other_weight = remote(
-        weight.at[1 - core], weight.at[1 - core], wp_send, wp_recv, peer
-    )
-    other_weight.wait_recv()
-
-    def term(t, at):
-        for k in range(2):
-            remote(
-                gathered.at[k, t], gathered.at[k, t], att_send.at[t, k], att_recv.at[k, t], peer
-            ).wait_recv()
-        left = jnp.concatenate([gathered[0, t], gathered[1, t]], axis=1)
-        for n in range(width // COLS):
+    kept.wait()
+    near_out.wait_recv()
+
+    def term(q, t, at):
+        if q == 0:
+            hand_over(t).wait_recv()
+            left = [placed[t, pl.ds(pl.multiple_of(core * rows, rows), rows), :], beside[t]]
+        else:
+            for k in range(2):
+                remote(
+                    gathered.at[k, t], gathered.at[k, t], att_send.at[t, k], att_recv.at[k, t],
+                    peer,
+                ).wait_recv()
+            left = [gathered[0, t], gathered[1, t]]
+        for n in range(mid // COLS):
             cut = slice(n * COLS, (n + 1) * COLS)
-            total[at, :, cut] = jnp.dot(
-                left, weight[:, :, cut].reshape(2 * DH, COLS), preferred_element_type=F32
+            total[q, at, :, cut] = jnp.dot(
+                jnp.concatenate(left, axis=1),
+                (near, far)[q][:, :, cut].reshape(2 * DH, COLS),
+                preferred_element_type=F32,
             )
 
-    def reduce_on(t, s):
-        cut = pl.ds(s * part, part)
-        return remote(
-            rs_out.at[t, cut], rs_in.at[t, cut], rs_send.at[t, s], rs_recv.at[t, s], toward(t)
-        )
-
-    def pass_on(t, at, s, first):
-        cut = pl.ds(s * part, part)
-        value = total[at, cut, :]
+    def reduce_on(q, t, s):
+        cut = pl.ds(s * part, part)
+        return remote(
+            rs_out.at[q, t, cut], rs_in.at[q, t, cut],
+            rs_send.at[q, t, s], rs_recv.at[q, t, s], toward(t),
+        )
+
+    def pass_on(q, t, at, s, first):
+        cut = pl.ds(s * part, part)
+        running = total[q, at, cut, :]
         if not first:
-            reduce_on(t - 2, s).wait_recv()
-            value += rs_in[t - 2, cut, :].astype(F32)
-        rs_out[t, cut, :] = value.astype(BF)
-        reduce_on(t, s).start()
-
-    for t in range(2):
-        term(t, t)
+            reduce_on(q, t - 2, s).wait_recv()
+            running += rs_in[q, t - 2, cut, :].astype(F32)
+        rs_out[q, t, cut, :] = running.astype(BF)
+        reduce_on(q, t, s).start()
+
+    def begin(q):
+        for t in range(2):
+            term(q, t, t)
+            for s in range(SUBS):
+                pass_on(q, t, t, s, True)
+
+    def keep_on(q):
+        @pl.loop(1, half - 1)
+        def _(p):
+            for t in range(2):
+                term(q, 2 * p + t, t)
+            for s in range(SUBS):
+                for t in range(2):
+                    pass_on(q, 2 * p + t, t, s, False)
+
+        for t in range(2):
+            term(q, n_chips - 2 + t, t)
         for s in range(SUBS):
-            pass_on(t, t, s, True)
-
-    @pl.loop(1, half - 1)
-    def _(p):
-        for t in range(2):
-            term(2 * p + t, t)
+            pass_on(q, n_chips - 2, 0, s, False)
+
+    def branch_of(q, s):
+        cut = pl.ds(s * part, part)
+        branch = total[q, 1, cut, :]
+        for t in (n_chips - 3, n_chips - 2):
+            reduce_on(q, t, s).wait_recv()
+            branch += rs_in[q, t, cut, :].astype(F32)
+        return branch
+
+    def send_early(s):
+        cut = pl.ds(s * part, part)
+        return remote(
+            ready.at[cut], early.at[cut], early_send.at[s], early_recv.at[s], straight
+        )
+
+    begin(0)
+    keep_on(0)
+    if LATE:
         for s in range(SUBS):
-            for t in range(2):
-                pass_on(2 * p + t, t, s, False)
-
-    for t in range(2):
-        term(n_chips - 2 + t, t)
-    for s in range(SUBS):
-        pass_on(n_chips - 2, 0, s, False)
+            ready[pl.ds(s * part, part), :] = branch_of(0, s).astype(BF)
+            send_early(s).start()
+    for k in range(2):
+        far_in(k).wait_recv()
+    begin(1)
+    if not LATE:
+        for s in range(SUBS):
+            ready[pl.ds(s * part, part), :] = branch_of(0, s).astype(BF)
+            send_early(s).start()
+    keep_on(1)
 
     def gather_on(u, s):
         cut = pl.ds(s * part, part)
@@ -276,10 +332,8 @@
     stream_out.wait_recv()
     for s in range(SUBS):
         cut = pl.ds(s * part, part)
-        branch = total[1, cut, :]
-        for t in (n_chips - 3, n_chips - 2):
-            reduce_on(t, s).wait_recv()
-            branch += rs_in[t, cut, :].astype(F32)
+        send_early(s).wait_recv()
+        branch = jnp.concatenate([early[cut, :].astype(F32), branch_of(1, s)], axis=1)
         after = (stream[cut, :].astype(F32) + branch).astype(BF)
         incoming_ref[cut, :] = after
         widened = after.astype(F32)
@@ -337,8 +391,11 @@
     for a in range(half):
         round_of(a, a == half - 1)
 
-    weight_out.wait_send()
-    weight_pair.wait_send()
+    near_out.wait_send()
+    for k in range(2):
+        far_out(k).wait_send()
+    for s in range(SUBS):
+        send_early(s).wait_send()
     stream_out.wait_send()
 
     @pl.loop(1, n_seq)
@@ -350,11 +407,13 @@
     def _(t):
         for k in range(2):
             hand_on(t, k).wait_send()
+        hand_over(t).wait_send()
 
     @pl.loop(0, n_chips - 1)
     def _(t):
         for s in range(SUBS):
-            reduce_on(t, s).wait_send()
+            for q in range(2):
+                reduce_on(q, t, s).wait_send()
             gather_on(t, s).wait_send()
             share(t, s).wait_send()
 
@@ -416,19 +475,25 @@
             pltpu.VMEM((tokens, tokens), F32),
             pltpu.VMEM((n_seq, rows, tokens), BF),
             pltpu.VMEM((n_chips, 2 * rows, DH), BF),
+            pltpu.VMEM((n_chips, rows, DH), BF),
             pltpu.VMEM((2, n_chips, rows, DH), BF),
-            pltpu.VMEM((2, DH, width), BF),
+            pltpu.VMEM((2, DH, width // 2), BF),
+            pltpu.VMEM((2, DH, width // 2), BF),
             pltpu.VMEM((rows, width), BF),
             pltpu.VMEM((width, head_cols), BF),
-            pltpu.VMEM((2, rows, width), F32),
-            pltpu.VMEM((n_chips - 1, rows, width), BF),
-            pltpu.VMEM((n_chips - 1, rows, width), BF),
+            pltpu.VMEM((2, 2, rows, width // 2), F32),
+            pltpu.VMEM((2, n_chips - 1, rows, width // 2), BF),
+            pltpu.VMEM((2, n_chips - 1, rows, width // 2), BF),
+            pltpu.VMEM((rows, width // 2), BF),
+            pltpu.VMEM((rows, width // 2), BF),
             pltpu.VMEM((n_chips, rows, width), BF),
             pltpu.VMEM((n_chips, rows, width), BF),
             pltpu.VMEM((4 * rows, head_cols), F32),
-            dma((3,)), dma((2,)), dma, dma((2, n_seq)), dma((2, n_seq)), dma, dma, dma, dma, dma, dma,
-            dma((n_chips, 2)), dma((2, n_chips)),
-            dma((n_chips - 1, SUBS)), dma((n_chips - 1, SUBS)),
+            dma((3,)), dma((2,)), dma, dma((2, n_seq)), dma((2, n_seq)),
+            dma, dma, dma, dma((2,)), dma((2,)), dma, dma,
+            dma((n_chips,)), dma((n_chips,)), dma((n_chips, 2)), dma((2, n_chips)),
+            dma((SUBS,)), dma((SUBS,)),
+            dma((2, n_chips - 1, SUBS)), dma((2, n_chips - 1, SUBS)),
             dma((n_chips - 1, SUBS)), dma((n_chips - 1, SUBS)),
             dma((n_chips, SUBS)), dma((n_chips, SUBS)),
         ],

time: 93.9 us -> 89.4 us (0.952)
  Pallas kernels: 93.2 us -> 88.6 us
    pallas_call x1, Pallas kernels: 92.2 us -> 87.6 us  [local(): pl.pallas_call(functools.partial(kernel, n_seg, n_seq), out_shape=(pltpu....]
where the time goes in v4:
time: 89.4 us; the launch traced here: 89.2 us
  Pallas kernels  88.6 us (99%)
    pallas_call x1, Pallas kernels, local(): pl.pallas_call(functools.partial(kernel, n_seg, n_seq), out_shape=(pltpu....  87.6 us

profile of v4, /device:TPU:1, one launch (start us, length us, event | category | flops | bytes accessed | tf_op | source)
XLA Modules:
  0.0 89.2 jit_solution(9270624121849412272)
XLA Ops:
  0.6 87.6 %section_boundary.1 = (bf16[64,2048]{1,0:T(8,128)(2,1)S(1)}, bf16[1024,384]{1,0:T(8,128)(2,1)S(1)}) custom-call(s32[8,128]{1,0:T(8,128)} %bitcast.12, s32[2,2,4]{2,1,0:T(2,128)} %bitcast.13, f32[1,2048]{1,0:T(1,128)} %gain_in.1, bf16[64,6144]{1,0:T(8,128)(2,1)} %bitcast.9, bf16[64,2048]{1,0:T(8,128)(2,1)} %bitcast.11, bf16[128,2048]{1,0:T(8,128)(2,1)} %bitcast.10, ...), custom_call_target="tpu_custom_call" | custom-call | tf_op jit(solution)/shard_map/section_boundary/pallas_call | solution.py:450
  88.3 1.0 %write_out.1 = (bf16[64,2048]{1,0:T(8,128)(2,1)}, bf16[1024,384]{1,0:T(8,128)(2,1)}) custom-call(bf16[64,2048]{1,0:T(8,128)(2,1)S(1)} %get-tuple-element.6.incoming, bf16[1024,384]{1,0:T(8,128)(2,1)S(1)} %get-tuple-element.7.following), custom_call_target="tpu_custom_call" | custom-call | tf_op jit(solution)/shard_map/write_out/pallas_call | solution.py:511

commit v5 on v4

--- a/solution.py
+++ b/solution.py
@@ -12,7 +12,6 @@
 BLOCK = 128
 LANES = 128
 SUBS = 4
-LATE = 0
 COLS = 512
 HIDDEN = -1e30
 BF = jnp.bfloat16
@@ -273,23 +272,23 @@
             for s in range(SUBS):
                 pass_on(q, t, t, s, True)
 
+        @pl.loop(2, n_chips)
+        def _(t):
+            term(q, t, t)
+
     def keep_on(q):
         @pl.loop(1, half - 1)
         def _(p):
-            for t in range(2):
-                term(q, 2 * p + t, t)
             for s in range(SUBS):
                 for t in range(2):
-                    pass_on(q, 2 * p + t, t, s, False)
-
-        for t in range(2):
-            term(q, n_chips - 2 + t, t)
+                    pass_on(q, 2 * p + t, 2 * p + t, s, False)
+
         for s in range(SUBS):
-            pass_on(q, n_chips - 2, 0, s, False)
+            pass_on(q, n_chips - 2, n_chips - 2, s, False)
 
     def branch_of(q, s):
         cut = pl.ds(s * part, part)
-        branch = total[q, 1, cut, :]
+        branch = total[q, n_chips - 1, cut, :]
         for t in (n_chips - 3, n_chips - 2):
             reduce_on(q, t, s).wait_recv()
             branch += rs_in[q, t, cut, :].astype(F32)
@@ -303,17 +302,12 @@
 
     begin(0)
     keep_on(0)
-    if LATE:
-        for s in range(SUBS):
-            ready[pl.ds(s * part, part), :] = branch_of(0, s).astype(BF)
-            send_early(s).start()
     for k in range(2):
         far_in(k).wait_recv()
     begin(1)
-    if not LATE:
-        for s in range(SUBS):
-            ready[pl.ds(s * part, part), :] = branch_of(0, s).astype(BF)
-            send_early(s).start()
+    for s in range(SUBS):
+        ready[pl.ds(s * part, part), :] = branch_of(0, s).astype(BF)
+        send_early(s).start()
     keep_on(1)
 
     def gather_on(u, s):
@@ -481,7 +475,7 @@
             pltpu.VMEM((2, DH, width // 2), BF),
             pltpu.VMEM((rows, width), BF),
             pltpu.VMEM((width, head_cols), BF),
-            pltpu.VMEM((2, 2, rows, width // 2), F32),
+            pltpu.VMEM((2, n_chips, rows, width // 2), F32),
             pltpu.VMEM((2, n_chips - 1, rows, width // 2), BF),
             pltpu.VMEM((2, n_chips - 1, rows, width // 2), BF),
             pltpu.VMEM((rows, width // 2), BF),

time: 89.4 us -> 89.1 us (level)
  no operation moved by 1% of the time
where the time goes in v5:
time: 89.1 us; the launch traced here: 88.9 us
  Pallas kernels  88.3 us (99%)
    pallas_call x1, Pallas kernels, local(): pl.pallas_call(functools.partial(kernel, n_seg, n_seq), out_shape=(pltpu....  87.3 us

profile of v5, /device:TPU:1, one launch (start us, length us, event | category | flops | bytes accessed | tf_op | source)
XLA Modules:
  0.0 88.9 jit_solution(546966795129608308)
XLA Ops:
  0.6 87.3 %section_boundary.1 = (bf16[64,2048]{1,0:T(8,128)(2,1)S(1)}, bf16[1024,384]{1,0:T(8,128)(2,1)S(1)}) custom-call(s32[8,128]{1,0:T(8,128)} %bitcast.12, s32[2,2,4]{2,1,0:T(2,128)} %bitcast.13, f32[1,2048]{1,0:T(1,128)} %gain_in.1, bf16[64,6144]{1,0:T(8,128)(2,1)} %bitcast.9, bf16[64,2048]{1,0:T(8,128)(2,1)} %bitcast.11, bf16[128,2048]{1,0:T(8,128)(2,1)} %bitcast.10, ...), custom_call_target="tpu_custom_call" | custom-call | tf_op jit(solution)/shard_map/section_boundary/pallas_call | solution.py:444
  87.9 1.0 %write_out.1 = (bf16[64,2048]{1,0:T(8,128)(2,1)}, bf16[1024,384]{1,0:T(8,128)(2,1)}) custom-call(bf16[64,2048]{1,0:T(8,128)(2,1)S(1)} %get-tuple-element.6.incoming, bf16[1024,384]{1,0:T(8,128)(2,1)S(1)} %get-tuple-element.7.following), custom_call_target="tpu_custom_call" | custom-call | tf_op jit(solution)/shard_map/write_out/pallas_call | solution.py:505
